TPU v7x, 32 devices: a whole 2x2x4 slice. The times are simulated.
32 devices in a mesh: blk: 8 (over z, y), rhs: 4 (over x, core).
Axes of the slice: x: 2, y: 2, z: 4, core: 2. Of those that a mesh axis runs over, the one named last changes fastest.
Arguments:
- rhs: float32 [8, 8, 8, 256, 128], P(None, None, 'blk', 'rhs'), parts along dimension 3, may hold values from -6 to 6
- lower_tiles: bfloat16 [8, 8, 8, 3, 128, 128], P(None, None, 'blk'), may hold values from -0.25 to 0.25
- lower_block_columns: int32 [8, 8, 8, 3], P(None, None, 'blk'), may hold values from 0 to 511, as said below
- upper_tiles: bfloat16 [8, 8, 8, 3, 128, 128], P(None, None, 'blk'), may hold values from -0.25 to 0.25
- upper_cols: int32 [8, 8, 8, 3], P(None, None, 'blk'), may hold values from 0 to 511, as said below
- diag_inverse: bfloat16 [8, 8, 8, 128, 128], P(None, None, 'blk')
Outputs:
- solution: bfloat16 [8, 8, 8, 256, 128], P(None, None, 'blk', 'rhs'), parts along dimension 3
There are 4 independent parts, one for each index of `rhs`. A program takes and returns all parts, laid end to end along the dimension named above; an argument that names none is the same for every part. Nothing has to cross between parts.
Inputs may be any that keep to these rules, and one draw needn't show every extreme that they name: `lower_block_columns`: entry k of block row (l * 8 + m) * 8 + p is either that row's own number (an empty slot) or ((l - 1) * 8 + m) * 8 + (p + d) mod 8 with d one of -1, 0, 1; the nonempty slots of a row have distinct d; rows with l = 0 have only empty slots. `upper_cols`: entry k of block row (l * 8 + m) * 8 + p is either that row's own number (an empty slot) or ((l + 1) * 8 + m) * 8 + (p + d) mod 8 with d one of -1, 0, 1; the nonempty slots of a row have distinct d; rows with l = 7 have only empty slots.
All inputs are finite; a program needn't handle non-finite values.
Results may differ from a plain program's by a relative error of at most 0.015.
Values may be sent and summed in bfloat16 or wider, within the bound.
A program may use at most 64 MiB of HBM per device.

v0:
```python
import functools

import jax
import jax.numpy as jnp
from jax import lax
from jax.experimental import pallas as pl
from jax.experimental.pallas import tpu as pltpu
from jax.sharding import PartitionSpec as P

MESH = pl.DeviceIdType.MESH
CHUNKS = 8
VMEM_LIMIT = 52 * 2**20
RELAYED = 1


def product(x, tile):
    return lax.dot_general(x, tile, (((1,), (1,)), ((), ())), preferred_element_type=jnp.float32)


def sweep_kernel(
    n,
    chunks,
    lower_cols,
    upper_cols,
    rhs,
    lower,
    upper,
    inverse,
    out,
    rhs_v,
    lower_v,
    upper_v,
    inverse_v,
    y,
    x,
    from_near,
    from_far,
    load_sem,
    store_sem,
    send_sem,
    recv_sem,
):
    levels, rows, sides, block = rhs.shape
    slots = lower.shape[2]
    step = rows // chunks
    last = levels - 1
    me = lax.axis_index("blk")
    odd = lax.rem(me, 2)
    near = me + 1 - 2 * odd
    far = lax.rem(me + 2 * odd + n - 1, n)
    onward = lax.rem(me + 2 - 4 * odd + n, n)
    feeder = lax.rem(me - 2 + 4 * odd + n, n)

    def load(kind, level):
        source, target = ((rhs, rhs_v), (lower, lower_v), (upper, upper_v), (inverse, inverse_v))[kind]
        return pltpu.make_async_copy(source.at[level], target.at[level], load_sem.at[kind, level])

    def start_forward(level, carry):
        load(0, level).start()
        load(1, level).start()
        return carry

    def start_backward(i, carry):
        level = levels - 2 - i
        load(3, level).start()
        load(2, level).start()
        return carry

    load(0, 0).start()
    barrier = pltpu.get_barrier_semaphore()
    for device in (near, far, feeder) if RELAYED else (near, far):
        pl.semaphore_signal(barrier, inc=1, device_id={"blk": device}, device_id_type=MESH)
    lax.fori_loop(1, levels, start_forward, 0)
    load(3, levels - 1).start()
    lax.fori_loop(0, levels - 1, start_backward, 0)

    def group(turn, j):
        return lax.rem(turn * RELAYED + j, chunks) * step

    def remote(source, target, sweep, level, turn, j, kind, device):
        return pltpu.make_async_remote_copy(
            src_ref=source.at[level, pl.ds(group(turn, j), step)],
            dst_ref=target.at[sweep, level, pl.ds(group(turn, j), step)],
            send_sem=send_sem.at[sweep, level, j, kind],
            recv_sem=recv_sem.at[sweep, level, j, kind],
            device_id={"blk": device},
            device_id_type=MESH,
        )

    def to_near(own, sweep, level, turn, j):
        return remote(own, from_near, sweep, level, turn, j, 0, near)

    def to_far(own, sweep, level, turn, j):
        if j < RELAYED:
            return remote(from_near.at[sweep], from_far, sweep, level, turn, j, 1, onward)
        return remote(own, from_far, sweep, level, turn, j, 1, far)

    def send(own, sweep, level, turn, j):
        to_near(own, sweep, level, turn, j).start()
        if j >= RELAYED:
            to_far(own, sweep, level, turn, j).start()

    def relay(own, sweep, level, turn):
        for j in range(RELAYED):
            to_near(own, sweep, level, turn, j).wait_recv()
            to_far(own, sweep, level, turn, j).start()

    def receive(own, sweep, level, turn, j):
        if j >= RELAYED:
            to_near(own, sweep, level, turn, j).wait_recv()
        to_far(own, sweep, level, turn, j).wait_recv()

    def terms(acc, cols, tiles, centre, sweep, level, source, m):
        base = (source * rows + m) * n
        side = from_near[sweep, source, m]
        mid = centre[source, m]
        other = from_far[sweep, source, m]
        for k in range(slots):
            column = cols[level, k, 0, m]
            chosen = lax.select(column == base + far, other, jnp.zeros_like(other))
            chosen = lax.select(column == base + me, mid, chosen)
            chosen = lax.select(column == base + near, side, chosen)
            acc = acc - product(chosen, tiles[level, m, k])
        return acc

    load(0, 0).wait()
    y[0] = rhs_v[0].astype(jnp.bfloat16)
    pl.semaphore_wait(barrier, 3 if RELAYED else 2)
    for j in range(chunks):
        send(y, 0, 0, 0, j)
    relay(y, 0, 0, 0)

    def forward(level, carry):
        load(0, level).wait()
        load(1, level).wait()
        for j in range(chunks):
            receive(y, 0, level - 1, level - 1, (j + RELAYED) % chunks)
            for i in range(step):
                m = group(level, j) + i
                acc = terms(rhs_v[level, m], lower_cols, lower_v, y, 0, level, level - 1, m)
                y[level, m] = acc.astype(jnp.bfloat16)

            @pl.when(level < last)
            def _():
                send(y, 0, level, level, j)

        @pl.when(level < last)
        def _():
            relay(y, 0, level, level)

        return carry

    lax.fori_loop(1, levels, forward, 0)

    def store(level):
        return pltpu.make_async_copy(x.at[level], out.at[level], store_sem.at[level])

    load(3, last).wait()
    for j in range(chunks):
        for i in range(step):
            m = group(0, j) + i
            x[last, m] = product(y[last, m], inverse_v[last, m]).astype(jnp.bfloat16)
        send(x, 1, last, 0, j)
    store(last).start()
    relay(x, 1, last, 0)

    def backward(turn, carry):
        level = last - turn
        load(3, level).wait()
        load(2, level).wait()
        for j in range(chunks):
            receive(x, 1, level + 1, turn - 1, (j + RELAYED) % chunks)
            for i in range(step):
                m = group(turn, j) + i
                acc = terms(
                    y[level, m].astype(jnp.float32), upper_cols, upper_v, x, 1, level, level + 1, m
                )
                w = acc.astype(jnp.bfloat16)
                x[level, m] = product(w, inverse_v[level, m]).astype(jnp.bfloat16)

            @pl.when(level > 0)
            def _():
                send(x, 1, level, turn, j)

        store(level).start()

        @pl.when(level > 0)
        def _():
            relay(x, 1, level, turn)

        return carry

    lax.fori_loop(1, levels, backward, 0)

    def finish(turn, carry):
        for j in range(chunks):
            for own, sweep, level in ((y, 0, turn), (x, 1, last - turn)):
                to_near(own, sweep, level, turn, j).wait_send()
                to_far(own, sweep, level, turn, j).wait_send()
        store(turn).wait()
        return carry

    lax.fori_loop(0, last, finish, 0)
    store(last).wait()


def on_device(n, rhs, lower_tiles, lower_block_columns, upper_tiles, upper_cols, diag_inverse):
    rhs = rhs[:, :, 0]
    lower = lower_tiles[:, :, 0]
    upper = upper_tiles[:, :, 0]
    inverse = diag_inverse[:, :, 0]
    levels, rows, sides, block = rhs.shape
    chunks = CHUNKS if rows % CHUNKS == 0 else 1
    halo = pltpu.VMEM((2, levels, rows, sides, block), jnp.bfloat16)
    own = pltpu.VMEM((levels, rows, sides, block), jnp.bfloat16)
    any_space = pl.BlockSpec(memory_space=pl.ANY)
    small = pl.BlockSpec(memory_space=pltpu.SMEM)
    result = pl.pallas_call(
        functools.partial(sweep_kernel, n, chunks),
        out_shape=jax.ShapeDtypeStruct(rhs.shape, jnp.bfloat16),
        in_specs=[small, small, any_space, any_space, any_space, any_space],
        out_specs=any_space,
        scratch_shapes=[
            pltpu.VMEM(rhs.shape, rhs.dtype),
            pltpu.VMEM(lower.shape, lower.dtype),
            pltpu.VMEM(upper.shape, upper.dtype),
            pltpu.VMEM(inverse.shape, inverse.dtype),
            own,
            own,
            halo,
            halo,
            pltpu.SemaphoreType.DMA((4, levels)),
            pltpu.SemaphoreType.DMA((levels,)),
            pltpu.SemaphoreType.DMA((2, levels, chunks, 2)),
            pltpu.SemaphoreType.DMA((2, levels, chunks, 2)),
        ],
        compiler_params=pltpu.CompilerParams(collective_id=0, has_side_effects=True, vmem_limit_bytes=VMEM_LIMIT),
    )(
        lower_block_columns.transpose(0, 3, 2, 1),
        upper_cols.transpose(0, 3, 2, 1),
        rhs,
        lower,
        upper,
        inverse,
    )
    return result[:, :, None]


def solution(mesh):
    return jax.shard_map(
        functools.partial(on_device, mesh.shape["blk"]),
        mesh=mesh,
        in_specs=(
            P(None, None, "blk", "rhs", None),
            P(None, None, "blk", None, None, None),
            P(None, None, "blk", None),
            P(None, None, "blk", None, None, None),
            P(None, None, "blk", None),
            P(None, None, "blk", None, None),
        ),
        out_specs=P(None, None, "blk", "rhs", None),
        check_vma=False,
    )
```

profile of v0, /device:TPU:0, one launch (start us, length us, event | category | flops | bytes accessed | tf_op | source)
XLA Modules:
  0.0 93.2 jit_solution(15063075146530187091)
XLA Ops:
  0.0 0.0 copy-start
  0.0 0.7 copy-done
  0.7 0.0 copy-start.1
  0.7 0.7 copy-done.1
  1.4 90.8 %shard_map.64 = bf16[8,8,64,128]{3,2,1,0:T(8,128)(2,1)S(1)} custom-call(s32[8,3,1,8]{3,2,1,0:T(1,128)S(1)} %bitcast.10, s32[8,3,1,8]{3,2,1,0:T(1,128)S(1)} %bitcast.11, f32[8,8,64,128]{3,2,1,0:T(8,128)} %bitcast.14, bf16[8,8,3,128,128]{4,3,2,1,0:T(8,128)(2,1)} %bitcast.12, bf16[8,8,3,128,128]{4,3,2,1,0:T(8,128)(2,1)} %bitcast.13, ...), custom_call_target="tpu_custom_call" | custom-call | tf_op jit(solution)/shard_map/pallas_call | solution.py:218
  92.3 1.0 %copy.9 = bf16[8,8,1,64,128]{4,3,2,1,0:T(8,128)(2,1)} copy(bf16[8,8,1,64,128]{4,3,2,1,0:T(8,128)(2,1)S(1)} %bitcast.9) | data formatting | bytes 2097152
Async XLA Ops:
  0.0 0.7 copy-start
  0.7 0.7 copy-start.1
where the time goes:
time: 93.6 us; the launch traced here: 93.2 us
  Pallas kernels  90.8 us (97%)
  local copies, waits for them, and re-layouts  2.39 us (3%)
    pallas_call x1, Pallas kernels, on_device(): pl.pallas_call(functools.partial(sweep_kernel, n, chunks), out_shape=jax....  90.8 us
    unnamed x5, local copies, waits for them, and re-layouts  2.39 us

commit v1 on v0

v1 whole, which is shorter than its diff:
```python
import functools

import jax
import jax.numpy as jnp
from jax import lax
from jax.experimental import pallas as pl
from jax.experimental.pallas import tpu as pltpu
from jax.sharding import PartitionSpec as P

MESH = pl.DeviceIdType.MESH
VMEM_LIMIT = 52 * 2**20
AHEAD = 4


def product(x, tile):
    return lax.dot_general(x, tile, (((1,), (1,)), ((), ())), preferred_element_type=jnp.float32)


def sweep_kernel(
    n,
    parts,
    lower_cols,
    upper_cols,
    rhs,
    lower,
    upper,
    inverse,
    out,
    cols,
    rhs_v,
    rhs_b,
    lower_v,
    upper_v,
    inverse_v,
    chosen,
    acc,
    y,
    x,
    halo,
    rhs_sem,
    load_sem,
    cols_sem,
    tile_send,
    tile_recv,
    cols_send,
    cols_recv,
    side_send,
    side_recv,
    edge_send,
    row_send,
    row_recv,
    out_send,
    out_recv,
):
    levels, rows, sides, block = rhs.shape
    slots = lower.shape[2]
    owners = 2 * parts
    share = rows // owners
    last = levels - 1
    me = lax.axis_index("blk")
    part = lax.axis_index("rhs")
    half = lax.rem(me, 2)
    pair = me - half
    partner = pair + 1 - half
    owner = half * parts + part
    mine = owner * share
    others = range(1, owners)

    def other(k):
        return lax.rem(owner + k, owners)

    def device(first, s):
        return {"blk": first + s // parts, "rhs": lax.rem(s, parts)}

    def load_rhs(level):
        return pltpu.make_async_copy(rhs.at[level], rhs_v.at[level], rhs_sem.at[level])

    def load(kind, level):
        source, target = ((lower, lower_v), (upper, upper_v), (inverse, inverse_v))[kind]
        return pltpu.make_async_copy(
            source.at[level, pl.ds(mine, share)], target.at[level, half], load_sem.at[kind, level]
        )

    def load_cols(kind):
        return pltpu.make_async_copy((lower_cols, upper_cols)[kind], cols.at[kind, half], cols_sem.at[kind])

    def give_cols(kind):
        return pltpu.make_async_remote_copy(
            src_ref=(lower_cols, upper_cols)[kind],
            dst_ref=cols.at[kind, half],
            send_sem=cols_send.at[kind],
            recv_sem=cols_recv.at[kind],
            device_id={"blk": partner},
            device_id_type=MESH,
        )

    def give_tiles(kind, level):
        source, target = ((lower, lower_v), (upper, upper_v), (inverse, inverse_v))[kind]
        theirs = ((1 - half) * parts + part) * share
        return pltpu.make_async_remote_copy(
            src_ref=source.at[level, pl.ds(theirs, share)],
            dst_ref=target.at[level, half],
            send_sem=tile_send.at[kind, level],
            recv_sem=tile_recv.at[kind, level],
            device_id={"blk": partner},
            device_id_type=MESH,
        )

    def give_sides(level, k):
        s = other(k)
        return pltpu.make_async_remote_copy(
            src_ref=rhs_b.at[level, pl.ds(s * share, share)],
            dst_ref=y.at[level, :, owner],
            send_sem=side_send.at[level, s],
            recv_sem=side_recv.at[level, owner],
            device_id=device(pair, s),
            device_id_type=MESH,
        )

    def take_sides(level, k):
        s = other(k)
        pltpu.make_async_remote_copy(
            src_ref=rhs_b.at[level, pl.ds(s * share, share)],
            dst_ref=y.at[level, :, s],
            send_sem=side_send.at[level, s],
            recv_sem=side_recv.at[level, s],
            device_id=device(pair, s),
            device_id_type=MESH,
        ).wait_recv()

    def give_edge(s, i):
        beside = lax.rem(pair + 4 * half - 2 + n, n)
        return pltpu.make_async_remote_copy(
            src_ref=rhs_b.at[0, s * share + i],
            dst_ref=halo.at[0, 0, i, part, half],
            send_sem=edge_send.at[s, i],
            recv_sem=row_recv.at[0, 0, i, part, half],
            device_id=device(beside, s),
            device_id_type=MESH,
        )

    def give_row(own, sweep, level, i, j, way):
        return pltpu.make_async_remote_copy(
            src_ref=own.at[level, i, way * parts + j],
            dst_ref=halo.at[sweep, level, i, j, way],
            send_sem=row_send.at[sweep, level, i, j, way],
            recv_sem=row_recv.at[sweep, level, i, j, way],
            device_id={"blk": lax.rem(me + 4 * way - 2 + n, n)},
            device_id_type=MESH,
        )

    def give_out(level, k):
        s = other(k)
        return pltpu.make_async_remote_copy(
            src_ref=x.at[level, :, s],
            dst_ref=out.at[level, pl.ds(mine, share)],
            send_sem=out_send.at[level, s],
            recv_sem=out_recv.at[level, owner],
            device_id=device(pair, s),
            device_id_type=MESH,
        )

    def keep_out(level):
        return pltpu.make_async_copy(
            x.at[level, :, owner], out.at[level, pl.ds(mine, share)], out_send.at[level, owner]
        )

    def take_out(level, k):
        s = other(k)
        pltpu.make_async_remote_copy(
            src_ref=x.at[level, :, s],
            dst_ref=out.at[level, pl.ds(s * share, share)],
            send_sem=out_send.at[level, s],
            recv_sem=out_recv.at[level, s],
            device_id=device(pair, s),
            device_id_type=MESH,
        ).wait_recv()

    def each(first, end, action):
        def step(level, carry):
            action(level)
            return carry

        lax.fori_loop(first, end, step, 0)

    load_rhs(0).start()
    barrier = pltpu.get_barrier_semaphore()

    def greet(first, s):
        pl.semaphore_signal(barrier, inc=1, device_id=device(first, s), device_id_type=MESH)

    for s in range(owners):
        greet(lax.rem(pair + 4 * half - 2 + n, n), s)
    for s in range(parts):
        greet(lax.rem(pair + 2 - 4 * half + n, n), half * parts + s)
    for k in others:
        greet(pair, other(k))
    each(1, levels, lambda level: load_rhs(level).start())
    load_cols(0).start()
    load_cols(1).start()
    each(1, levels, lambda level: load(0, level).start())
    each(0, levels, lambda level: load(2, last - level).start())
    each(1, levels, lambda level: load(1, last - level).start())

    def narrow(level):
        load_rhs(level).wait()
        rhs_b[level] = rhs_v[level].astype(jnp.bfloat16)
        for i in range(share):
            y[level, i, owner] = rhs_v[level, mine + i].astype(jnp.bfloat16)

    each(0, levels, narrow)
    pl.semaphore_wait(barrier, 2 * owners + parts - 1)

    def forward_item(level):
        for k in others:
            give_sides(level, k).start()
        give_tiles(0, level).start()

    def backward_item(level):
        @pl.when(level < last)
        def _():
            give_tiles(1, level).start()

        give_tiles(2, level).start()

    def ahead_forward(level):
        @pl.when(level + AHEAD <= last)
        def _():
            forward_item(level + AHEAD)

        @pl.when(level + AHEAD > last)
        def _():
            backward_item(2 * last + 1 - AHEAD - level)

    def ahead_backward(turn):
        @pl.when(turn + AHEAD - 1 <= last)
        def _():
            backward_item(last - turn - AHEAD + 1)

    for s in range(owners):
        for i in range(share):
            give_edge(s, i).start()
    for k in others:
        give_sides(0, k).start()
    give_cols(0).start()
    give_cols(1).start()
    each(1, AHEAD + 1, forward_item)
    for k in others:
        take_sides(0, k)
    for kind in range(2):
        load_cols(kind).wait()
        give_cols(kind).wait_recv()

    def choose(sweep, level, source, tiles):
        for i in range(share):
            base = (source * rows + mine + i) * n
            for p in range(2):
                for d in range(3):
                    wanted = base + lax.rem(pair + p + d - 1 + n, n)
                    tile = jnp.zeros((block, block), tiles.dtype)
                    for k in range(slots):
                        found = cols[sweep, p, level, k, 0, mine + i] == wanted
                        tile = lax.select(found, tiles[level, p, i, k], tile)
                    chosen[i, p, d] = tile

    def early(sweep, level, source, own):
        for i in range(share):
            first = own[source, i, 0:parts].reshape(parts * sides, block)
            second = own[source, i, parts:owners].reshape(parts * sides, block)
            for p in range(2):
                start = y[level, i, p * parts : (p + 1) * parts].reshape(parts * sides, block)
                terms = product(first, chosen[i, p, 1 - p]) + product(second, chosen[i, p, 2 - p])
                acc[i, p] = (start.astype(jnp.float32) - terms).reshape(parts, sides, block)

    def late(own, sweep, source, i, j):
        for way in range(2):
            give_row(own, sweep, source, i, j, way).wait_recv()
        low = acc[i, 0, j] - product(halo[sweep, source, i, j, 1], chosen[i, 0, 0])
        high = acc[i, 1, j] - product(halo[sweep, source, i, j, 0], chosen[i, 1, 2])
        return low.astype(jnp.bfloat16), high.astype(jnp.bfloat16)

    def arrive_forward(level):
        for k in others:
            take_sides(level, k)
        load(0, level).wait()
        give_tiles(0, level).wait_recv()

    def forward(level):
        arrive_forward(level)
        choose(0, level, level - 1, lower_v)
        early(0, level, level - 1, y)
        for i in range(share):
            for j in range(parts):
                low, high = late(y, 0, level - 1, i, j)
                y[level, i, j] = low
                y[level, i, parts + j] = high
                for way in range(2):
                    give_row(y, 0, level, i, j, way).start()
        ahead_forward(level)

    each(1, last, forward)

    def solve(level, i, j, low, high):
        x[level, i, j] = product(low, inverse_v[level, 0, i]).astype(jnp.bfloat16)
        x[level, i, parts + j] = product(high, inverse_v[level, 1, i]).astype(jnp.bfloat16)

    def leave(level):
        for k in others:
            give_out(level, k).start()
        keep_out(level).start()

    arrive_forward(last)
    load(2, last).wait()
    give_tiles(2, last).wait_recv()
    choose(0, last, last - 1, lower_v)
    early(0, last, last - 1, y)
    for i in range(share):
        for j in range(parts):
            low, high = late(y, 0, last - 1, i, j)
            solve(last, i, j, low, high)
            for way in range(2):
                give_row(x, 1, last, i, j, way).start()
    ahead_forward(last)
    leave(last)

    def backward(turn):
        level = last - turn
        load(1, level).wait()
        give_tiles(1, level).wait_recv()
        load(2, level).wait()
        give_tiles(2, level).wait_recv()
        choose(1, level, level + 1, upper_v)
        early(1, level, level + 1, x)
        for i in range(share):
            for j in range(parts):
                low, high = late(x, 1, level + 1, i, j)
                solve(level, i, j, low, high)

                @pl.when(level > 0)
                def _():
                    for way in range(2):
                        give_row(x, 1, level, i, j, way).start()

        ahead_backward(turn)
        leave(level)

    each(1, levels, backward)

    for kind in range(2):
        give_cols(kind).wait_send()
    for s in range(owners):
        for i in range(share):
            give_edge(s, i).wait_send()

    def finish(level):
        for k in others:
            give_sides(level, k).wait_send()
            give_out(level, k).wait_send()
            take_out(level, k)
        keep_out(level).wait()
        give_tiles(2, level).wait_send()

    each(0, levels, finish)

    def finish_tiles(level):
        give_tiles(0, level).wait_send()
        give_tiles(1, level - 1).wait_send()
        for i in range(share):
            for j in range(parts):
                for way in range(2):
                    give_row(x, 1, level, i, j, way).wait_send()

    each(1, levels, finish_tiles)

    def finish_rows(level):
        for i in range(share):
            for j in range(parts):
                for way in range(2):
                    give_row(y, 0, level, i, j, way).wait_send()

    each(1, last, finish_rows)


def on_device(n, parts, rhs, lower_tiles, lower_block_columns, upper_tiles, upper_cols, diag_inverse):
    rhs = rhs[:, :, 0]
    lower = lower_tiles[:, :, 0]
    upper = upper_tiles[:, :, 0]
    inverse = diag_inverse[:, :, 0]
    levels, rows, sides, block = rhs.shape
    slots = lower.shape[2]
    owners = 2 * parts
    share = rows // owners
    half = jnp.bfloat16
    dma = pltpu.SemaphoreType.DMA
    any_space = pl.BlockSpec(memory_space=pl.ANY)
    tiles = pltpu.VMEM((levels, 2, share, slots, block, block), half)
    own = pltpu.VMEM((levels, share, owners, sides, block), half)
    result = pl.pallas_call(
        functools.partial(sweep_kernel, n, parts),
        out_shape=jax.ShapeDtypeStruct(rhs.shape, half),
        in_specs=[any_space] * 6,
        out_specs=any_space,
        scratch_shapes=[
            pltpu.SMEM((2, 2, levels, slots, 1, rows), jnp.int32),
            pltpu.VMEM(rhs.shape, rhs.dtype),
            pltpu.VMEM(rhs.shape, half),
            tiles,
            tiles,
            pltpu.VMEM((levels, 2, share, block, block), half),
            pltpu.VMEM((share, 2, 3, block, block), half),
            pltpu.VMEM((share, 2, parts, sides, block), jnp.float32),
            own,
            own,
            pltpu.VMEM((2, levels, share, parts, 2, sides, block), half),
            dma((levels,)),
            dma((3, levels)),
            dma((2,)),
            dma((3, levels)),
            dma((3, levels)),
            dma((2,)),
            dma((2,)),
            dma((levels, owners)),
            dma((levels, owners)),
            dma((owners, share)),
            dma((2, levels, share, parts, 2)),
            dma((2, levels, share, parts, 2)),
            dma((levels, owners)),
            dma((levels, owners)),
        ],
        compiler_params=pltpu.CompilerParams(collective_id=0, has_side_effects=True, vmem_limit_bytes=VMEM_LIMIT),
    )(
        lower_block_columns.transpose(0, 3, 2, 1),
        upper_cols.transpose(0, 3, 2, 1),
        rhs,
        lower,
        upper,
        inverse,
    )
    return result[:, :, None]


def solution(mesh):
    return jax.shard_map(
        functools.partial(on_device, mesh.shape["blk"], mesh.shape["rhs"]),
        mesh=mesh,
        in_specs=(
            P(None, None, "blk", "rhs", None),
            P(None, None, "blk", None, None, None),
            P(None, None, "blk", None),
            P(None, None, "blk", None, None, None),
            P(None, None, "blk", None),
            P(None, None, "blk", None, None),
        ),
        out_specs=P(None, None, "blk", "rhs", None),
        check_vma=False,
    )
```

time: 93.6 us -> 84.3 us (0.901)
  Pallas kernels: 90.8 us -> 81.6 us
    pallas_call x1, Pallas kernels: 90.8 us -> 81.6 us  [on_device(): pl.pallas_call(functools.partial(sweep_kernel, n, parts), out_shape=jax.S...]
where the time goes in v1:
time: 84.3 us; the launch traced here: 84 us
  Pallas kernels  81.6 us (97%)
  local copies, waits for them, and re-layouts  2.39 us (3%)
    pallas_call x1, Pallas kernels, on_device(): pl.pallas_call(functools.partial(sweep_kernel, n, parts), out_shape=jax.S...  81.6 us
    unnamed x5, local copies, waits for them, and re-layouts  2.39 us

profile of v1, /device:TPU:0, one launch (start us, length us, event | category | flops | bytes accessed | tf_op | source)
XLA Modules:
  0.0 84.0 jit_solution(5169297621549283027)
XLA Ops:
  0.0 0.0 copy-start
  0.0 0.7 copy-done
  0.7 0.0 copy-start.1
  0.7 0.7 copy-done.1
  1.4 81.6 %shard_map.64 = bf16[8,8,64,128]{3,2,1,0:T(8,128)(2,1)S(1)} custom-call(s32[8,3,1,8]{3,2,1,0:T(1,128)S(1)} %bitcast.10, s32[8,3,1,8]{3,2,1,0:T(1,128)S(1)} %bitcast.11, f32[8,8,64,128]{3,2,1,0:T(8,128)} %bitcast.14, bf16[8,8,3,128,128]{4,3,2,1,0:T(8,128)(2,1)} %bitcast.12, bf16[8,8,3,128,128]{4,3,2,1,0:T(8,128)(2,1)} %bitcast.13, ...), custom_call_target="tpu_custom_call" | custom-call | tf_op jit(solution)/shard_map/pallas_call | solution.py:398
  83.0 1.0 %copy.9 = bf16[8,8,1,64,128]{4,3,2,1,0:T(8,128)(2,1)} copy(bf16[8,8,1,64,128]{4,3,2,1,0:T(8,128)(2,1)S(1)} %bitcast.9) | data formatting | bytes 2097152
Async XLA Ops:
  0.0 0.7 copy-start
  0.7 0.7 copy-start.1

commit v2 on v1

v2 whole, which is shorter than its diff:
```python
import functools

import jax
import jax.numpy as jnp
from jax import lax
from jax.experimental import pallas as pl
from jax.experimental.pallas import tpu as pltpu
from jax.sharding import PartitionSpec as P

MESH = pl.DeviceIdType.MESH
VMEM_LIMIT = 52 * 2**20
AHEAD = 4


def product(x, tile):
    return lax.dot_general(x, tile, (((1,), (1,)), ((), ())), preferred_element_type=jnp.float32)


def sweep_kernel(
    n,
    parts,
    lower_cols,
    upper_cols,
    rhs,
    lower,
    upper,
    inverse,
    out,
    cols,
    rhs_v,
    rhs_b,
    lower_v,
    upper_v,
    inverse_v,
    chosen,
    acc,
    y,
    x,
    halo,
    rhs_sem,
    load_sem,
    cols_sem,
    tile_send,
    tile_recv,
    side_send,
    side_recv,
    edge_send,
    row_send,
    row_recv,
    out_sem,
):
    levels, rows, sides, block = rhs.shape
    slots = lower.shape[2]
    owners = 2 * parts
    share = rows // owners
    last = levels - 1
    me = lax.axis_index("blk")
    part = lax.axis_index("rhs")
    half = lax.rem(me, 2)
    pair = me - half
    partner = pair + 1 - half
    owner = half * parts + part
    mine = owner * share
    others = range(1, owners)

    def other(k):
        return lax.rem(owner + k, owners)

    def device(first, s):
        return {"blk": first + s // parts, "rhs": lax.rem(s, parts)}

    def load_rhs(first, count):
        span = pl.ds(first, count)
        return pltpu.make_async_copy(rhs.at[span], rhs_v.at[span], rhs_sem.at[min(first, 1)])

    def tiles_of(kind):
        return ((lower, lower_v), (upper, upper_v), (inverse, inverse_v))[kind]

    spans = (pl.ds(1, last), pl.ds(0, last), pl.ds(0, levels))

    def load(kind):
        source, target = tiles_of(kind)
        span = spans[kind]
        return pltpu.make_async_copy(
            source.at[span, pl.ds(mine, share)], target.at[span, half], load_sem.at[kind]
        )

    def load_cols(kind):
        return pltpu.make_async_copy((lower_cols, upper_cols)[kind], cols.at[half, kind], cols_sem.at[0, kind])

    def remote(source, target, send_sem, recv_sem, device_id):
        return pltpu.make_async_remote_copy(
            src_ref=source,
            dst_ref=target,
            send_sem=send_sem,
            recv_sem=recv_sem,
            device_id=device_id,
            device_id_type=MESH,
        )

    def give_cols(kind):
        return remote(
            (lower_cols, upper_cols)[kind],
            cols.at[half, kind],
            cols_sem.at[1, kind],
            cols_sem.at[2, kind],
            {"blk": partner},
        )

    def give_tiles(kind, level):
        source, target = tiles_of(kind)
        theirs = ((1 - half) * parts + part) * share
        return remote(
            source.at[level, pl.ds(theirs, share)],
            target.at[level, half],
            tile_send.at[kind],
            tile_recv.at[kind, level],
            {"blk": partner},
        )

    def tiles_given(kind):
        source, target = tiles_of(kind)
        span = spans[kind]
        remote(
            source.at[span, pl.ds(0, share)], target.at[span, half], tile_send.at[kind], tile_recv.at[kind, 0], {"blk": partner}
        ).wait_send()

    def give_sides(level, k):
        s = other(k)
        return remote(
            rhs_b.at[level, pl.ds(s * share, share)],
            y.at[level, :, owner],
            side_send.at[0],
            side_recv.at[level],
            device(pair, s),
        )

    def sides_given():
        whole = rhs_b.at[:, pl.ds(0, rows - share)]
        remote(whole, whole, side_send.at[0], side_recv.at[0], {"blk": partner}).wait_send()

    def take_sides(level):
        whole = y.at[level, :, pl.ds(0, owners - 1)]
        remote(whole, whole, side_send.at[0], side_recv.at[level], {"blk": partner}).wait_recv()

    def give_edge(s, i):
        beside = lax.rem(pair + 4 * half - 2 + n, n)
        return remote(
            rhs_b.at[0, s * share + i],
            halo.at[0, 0, i, part, half],
            edge_send.at[0],
            row_recv.at[0, i, part],
            device(beside, s),
        )

    def edges_given():
        remote(rhs_b.at[0], rhs_b.at[0], edge_send.at[0], row_recv.at[0, 0, 0], {"blk": partner}).wait_send()

    def turn_of(sweep, level):
        return lax.rem(level if sweep == 0 else 2 * last - level, 2)

    def give_row(own, sweep, level, i, j, way):
        return remote(
            own.at[level, i, way * parts + j],
            halo.at[sweep, level, i, j, way],
            row_send.at[sweep],
            row_recv.at[turn_of(sweep, level), i, j],
            {"blk": lax.rem(me + 4 * way - 2 + n, n)},
        )

    def take_rows(sweep, level, i, j):
        whole = halo.at[sweep, level, i, j]
        remote(
            whole, whole, row_send.at[sweep], row_recv.at[turn_of(sweep, level), i, j], {"blk": partner}
        ).wait_recv()

    def rows_given(own, sweep, count):
        whole = own.at[pl.ds(1, count)]
        remote(whole, whole, row_send.at[sweep], row_recv.at[0, 0, 0], {"blk": partner}).wait_send()

    def give_out(level, k):
        s = other(k)
        return remote(
            x.at[level, :, s],
            out.at[level, pl.ds(mine, share)],
            out_sem.at[0],
            out_sem.at[1],
            device(pair, s),
        )

    def keep_out(level):
        return pltpu.make_async_copy(x.at[level, :, owner], out.at[level, pl.ds(mine, share)], out_sem.at[2])

    def outs_done():
        sent = x.at[:, :, pl.ds(0, owners - 1)]
        kept = x.at[:, :, owner]
        got = out.at[:, pl.ds(0, rows - share)]
        pltpu.make_async_copy(kept, out.at[:, pl.ds(mine, share)], out_sem.at[2]).wait()
        remote(sent, sent, out_sem.at[0], out_sem.at[1], {"blk": partner}).wait_send()
        remote(got, got, out_sem.at[0], out_sem.at[1], {"blk": partner}).wait_recv()

    def each(first, end, action):
        def step(level, carry):
            action(level)
            return carry

        lax.fori_loop(first, end, step, 0)

    load_rhs(0, 1).start()
    barrier = pltpu.get_barrier_semaphore()

    def greet(first, s):
        pl.semaphore_signal(barrier, inc=1, device_id=device(first, s), device_id_type=MESH)

    for s in range(owners):
        greet(lax.rem(pair + 4 * half - 2 + n, n), s)
    for s in range(parts):
        greet(lax.rem(pair + 2 - 4 * half + n, n), half * parts + s)
    for k in others:
        greet(pair, other(k))
    load_rhs(1, last).start()
    for kind in range(2):
        load_cols(kind).start()
    for kind in range(3):
        load(kind).start()

    def narrow(level):
        rhs_b[level] = rhs_v[level].astype(jnp.bfloat16)
        for i in range(share):
            y[level, i, owner] = rhs_v[level, mine + i].astype(jnp.bfloat16)

    load_rhs(0, 1).wait()
    narrow(0)
    pl.semaphore_wait(barrier, 2 * owners + parts - 1)
    for k in others:
        give_sides(0, k).start()
    for s in range(owners):
        for i in range(share):
            give_edge(s, i).start()
    give_cols(0).start()
    give_cols(1).start()

    def forward_item(level):
        for k in others:
            give_sides(level, k).start()
        give_tiles(0, level).start()

    def backward_item(level):
        @pl.when(level < last)
        def _():
            give_tiles(1, level).start()

        give_tiles(2, level).start()

    def ahead_forward(level):
        @pl.when(level + AHEAD <= last)
        def _():
            forward_item(level + AHEAD)

        @pl.when(level + AHEAD > last)
        def _():
            backward_item(2 * last + 1 - AHEAD - level)

    def ahead_backward(turn):
        @pl.when(turn + AHEAD - 1 <= last)
        def _():
            backward_item(last - turn - AHEAD + 1)

    def open_item(level):
        narrow(level)
        forward_item(level)

    load_rhs(1, last).wait()
    each(1, AHEAD + 1, open_item)
    each(AHEAD + 1, levels, narrow)
    take_sides(0)
    for kind in range(2):
        load_cols(kind).wait()
        give_cols(kind).wait_recv()
    for kind in range(3):
        load(kind).wait()

    def choose(sweep, level, source, tiles):
        for i in range(share):
            base = (source * rows + mine + i) * n
            for p in range(2):
                for d in range(3):
                    wanted = base + lax.rem(pair + p + d - 1 + n, n)
                    tile = jnp.zeros((block, block), tiles.dtype)
                    for k in range(slots):
                        found = cols[p, sweep, level, k, 0, mine + i] == wanted
                        tile = lax.select(found, tiles[level, p, i, k], tile)
                    chosen[i, p, d] = tile

    def early(sweep, level, source, own):
        for i in range(share):
            first = own[source, i, 0:parts].reshape(parts * sides, block)
            second = own[source, i, parts:owners].reshape(parts * sides, block)
            for p in range(2):
                start = y[level, i, p * parts : (p + 1) * parts].reshape(parts * sides, block)
                terms = product(first, chosen[i, p, 1 - p]) + product(second, chosen[i, p, 2 - p])
                acc[i, p] = (start.astype(jnp.float32) - terms).reshape(parts, sides, block)

    def late(own, sweep, source, i, j):
        take_rows(sweep, source, i, j)
        low = acc[i, 0, j] - product(halo[sweep, source, i, j, 1], chosen[i, 0, 0])
        high = acc[i, 1, j] - product(halo[sweep, source, i, j, 0], chosen[i, 1, 2])
        return low.astype(jnp.bfloat16), high.astype(jnp.bfloat16)

    def arrive_forward(level):
        take_sides(level)
        give_tiles(0, level).wait_recv()

    def forward(level):
        arrive_forward(level)
        choose(0, level, level - 1, lower_v)
        early(0, level, level - 1, y)
        for i in range(share):
            for j in range(parts):
                low, high = late(y, 0, level - 1, i, j)
                y[level, i, j] = low
                y[level, i, parts + j] = high
                for way in range(2):
                    give_row(y, 0, level, i, j, way).start()
        ahead_forward(level)

    each(1, last, forward)

    def solve(level, i, j, low, high):
        x[level, i, j] = product(low, inverse_v[level, 0, i]).astype(jnp.bfloat16)
        x[level, i, parts + j] = product(high, inverse_v[level, 1, i]).astype(jnp.bfloat16)

    def leave(level):
        for k in others:
            give_out(level, k).start()
        keep_out(level).start()

    arrive_forward(last)
    give_tiles(2, last).wait_recv()
    choose(0, last, last - 1, lower_v)
    early(0, last, last - 1, y)
    for i in range(share):
        for j in range(parts):
            low, high = late(y, 0, last - 1, i, j)
            solve(last, i, j, low, high)
            for way in range(2):
                give_row(x, 1, last, i, j, way).start()
    ahead_forward(last)
    leave(last)

    def backward(turn):
        level = last - turn
        give_tiles(1, level).wait_recv()
        give_tiles(2, level).wait_recv()
        choose(1, level, level + 1, upper_v)
        early(1, level, level + 1, x)
        for i in range(share):
            for j in range(parts):
                low, high = late(x, 1, level + 1, i, j)
                solve(level, i, j, low, high)

                @pl.when(level > 0)
                def _():
                    for way in range(2):
                        give_row(x, 1, level, i, j, way).start()

        ahead_backward(turn)
        leave(level)

    each(1, levels, backward)

    for kind in range(2):
        give_cols(kind).wait_send()
    edges_given()
    sides_given()
    rows_given(y, 0, last - 1)
    rows_given(x, 1, last)
    for kind in range(3):
        tiles_given(kind)
    outs_done()


def on_device(n, parts, rhs, lower_tiles, lower_block_columns, upper_tiles, upper_cols, diag_inverse):
    rhs = rhs[:, :, 0]
    lower = lower_tiles[:, :, 0]
    upper = upper_tiles[:, :, 0]
    inverse = diag_inverse[:, :, 0]
    levels, rows, sides, block = rhs.shape
    slots = lower.shape[2]
    owners = 2 * parts
    share = rows // owners
    half = jnp.bfloat16
    dma = pltpu.SemaphoreType.DMA
    any_space = pl.BlockSpec(memory_space=pl.ANY)
    tiles = pltpu.VMEM((levels, 2, share, slots, block, block), half)
    own = pltpu.VMEM((levels, share, owners, sides, block), half)
    result = pl.pallas_call(
        functools.partial(sweep_kernel, n, parts),
        out_shape=jax.ShapeDtypeStruct(rhs.shape, half),
        in_specs=[pl.BlockSpec(memory_space=pltpu.HBM)] * 6,
        out_specs=any_space,
        scratch_shapes=[
            pltpu.SMEM((2, 2, levels, slots, 1, rows), jnp.int32),
            pltpu.VMEM(rhs.shape, rhs.dtype),
            pltpu.VMEM(rhs.shape, half),
            tiles,
            tiles,
            pltpu.VMEM((levels, 2, share, block, block), half),
            pltpu.VMEM((share, 2, 3, block, block), half),
            pltpu.VMEM((share, 2, parts, sides, block), jnp.float32),
            own,
            own,
            pltpu.VMEM((2, levels, share, parts, 2, sides, block), half),
            dma((2,)),
            dma((3,)),
            dma((3, 2)),
            dma((3,)),
            dma((3, levels)),
            dma((1,)),
            dma((levels,)),
            dma((1,)),
            dma((2,)),
            dma((2, share, parts)),
            dma((3,)),
        ],
        compiler_params=pltpu.CompilerParams(collective_id=0, has_side_effects=True, vmem_limit_bytes=VMEM_LIMIT),
    )(
        lower_block_columns.transpose(0, 3, 2, 1),
        upper_cols.transpose(0, 3, 2, 1),
        rhs,
        lower,
        upper,
        inverse,
    )
    return result[:, :, None]


def solution(mesh):
    return jax.shard_map(
        functools.partial(on_device, mesh.shape["blk"], mesh.shape["rhs"]),
        mesh=mesh,
        in_specs=(
            P(None, None, "blk", "rhs", None),
            P(None, None, "blk", None, None, None),
            P(None, None, "blk", None),
            P(None, None, "blk", None, None, None),
            P(None, None, "blk", None),
            P(None, None, "blk", None, None),
        ),
        out_specs=P(None, None, "blk", "rhs", None),
        check_vma=False,
    )
```

time: 84.3 us -> 79 us (0.937)
  Pallas kernels: 81.6 us -> 76.3 us
    pallas_call x1, Pallas kernels: 81.6 us -> 76.3 us  [on_device(): pl.pallas_call(functools.partial(sweep_kernel, n, parts), out_shape=jax.S...]
where the time goes in v2:
time: 79 us; the launch traced here: 78.7 us
  Pallas kernels  76.3 us (97%)
  local copies, waits for them, and re-layouts  2.39 us (3%)
    pallas_call x1, Pallas kernels, on_device(): pl.pallas_call(functools.partial(sweep_kernel, n, parts), out_shape=jax.S...  76.3 us
    unnamed x5, local copies, waits for them, and re-layouts  2.39 us

profile of v2, /device:TPU:0, one launch (start us, length us, event | category | flops | bytes accessed | tf_op | source)
XLA Modules:
  0.0 78.7 jit_solution(3773936661579915568)
XLA Ops:
  0.0 0.0 copy-start
  0.0 0.7 copy-done
  0.7 0.0 copy-start.1
  0.7 0.7 copy-done.1
  1.4 76.3 %shard_map.64 = bf16[8,8,64,128]{3,2,1,0:T(8,128)(2,1)S(1)} custom-call(s32[8,3,1,8]{3,2,1,0:T(1,128)S(1)} %bitcast.10, s32[8,3,1,8]{3,2,1,0:T(1,128)S(1)} %bitcast.11, f32[8,8,64,128]{3,2,1,0:T(8,128)} %bitcast.14, bf16[8,8,3,128,128]{4,3,2,1,0:T(8,128)(2,1)} %bitcast.12, bf16[8,8,3,128,128]{4,3,2,1,0:T(8,128)(2,1)} %bitcast.13, ...), custom_call_target="tpu_custom_call" | custom-call | tf_op jit(solution)/shard_map/pallas_call | solution.py:397
  77.7 1.0 %copy.9 = bf16[8,8,1,64,128]{4,3,2,1,0:T(8,128)(2,1)} copy(bf16[8,8,1,64,128]{4,3,2,1,0:T(8,128)(2,1)S(1)} %bitcast.9) | data formatting | bytes 2097152
Async XLA Ops:
  0.0 0.7 copy-start
  0.7 0.7 copy-start.1

commit v3 on v2

--- a/solution.py
+++ b/solution.py
@@ -8,7 +8,7 @@
 from jax.sharding import PartitionSpec as P
 
 MESH = pl.DeviceIdType.MESH
-VMEM_LIMIT = 52 * 2**20
+VMEM_LIMIT = 67043328
 AHEAD = 4
 
 
@@ -33,7 +33,6 @@
     upper_v,
     inverse_v,
     chosen,
-    acc,
     y,
     x,
     halo,
@@ -44,7 +43,6 @@
     tile_recv,
     side_send,
     side_recv,
-    edge_send,
     row_send,
     row_recv,
     out_sem,
@@ -143,19 +141,6 @@
         whole = y.at[level, :, pl.ds(0, owners - 1)]
         remote(whole, whole, side_send.at[0], side_recv.at[level], {"blk": partner}).wait_recv()
 
-    def give_edge(s, i):
-        beside = lax.rem(pair + 4 * half - 2 + n, n)
-        return remote(
-            rhs_b.at[0, s * share + i],
-            halo.at[0, 0, i, part, half],
-            edge_send.at[0],
-            row_recv.at[0, i, part],
-            device(beside, s),
-        )
-
-    def edges_given():
-        remote(rhs_b.at[0], rhs_b.at[0], edge_send.at[0], row_recv.at[0, 0, 0], {"blk": partner}).wait_send()
-
     def turn_of(sweep, level):
         return lax.rem(level if sweep == 0 else 2 * last - level, 2)
 
@@ -174,22 +159,32 @@
             whole, whole, row_send.at[sweep], row_recv.at[turn_of(sweep, level), i, j], {"blk": partner}
         ).wait_recv()
 
-    def rows_given(own, sweep, count):
-        whole = own.at[pl.ds(1, count)]
+    def rows_given(own, sweep):
+        whole = own.at[pl.ds(sweep, last)]
         remote(whole, whole, row_send.at[sweep], row_recv.at[0, 0, 0], {"blk": partner}).wait_send()
 
-    def give_out(level, k):
-        s = other(k)
+    def give_out(level, i, s):
         return remote(
-            x.at[level, :, s],
-            out.at[level, pl.ds(mine, share)],
+            x.at[level, i, s],
+            out.at[level, mine + i],
             out_sem.at[0],
             out_sem.at[1],
             device(pair, s),
         )
 
-    def keep_out(level):
-        return pltpu.make_async_copy(x.at[level, :, owner], out.at[level, pl.ds(mine, share)], out_sem.at[2])
+    def keep_out(level, i):
+        return pltpu.make_async_copy(x.at[level, i, owner], out.at[level, mine + i], out_sem.at[2])
+
+    def leave_piece(level, i, j):
+        for s in (j, parts + j):
+
+            @pl.when(owner != s)
+            def _():
+                give_out(level, i, s).start()
+
+            @pl.when(owner == s)
+            def _():
+                keep_out(level, i).start()
 
     def outs_done():
         sent = x.at[:, :, pl.ds(0, owners - 1)]
@@ -212,10 +207,10 @@
     def greet(first, s):
         pl.semaphore_signal(barrier, inc=1, device_id=device(first, s), device_id_type=MESH)
 
-    for s in range(owners):
-        greet(lax.rem(pair + 4 * half - 2 + n, n), s)
-    for s in range(parts):
-        greet(lax.rem(pair + 2 - 4 * half + n, n), half * parts + s)
+    for way in range(2):
+        pl.semaphore_signal(
+            barrier, inc=1, device_id={"blk": lax.rem(me + 4 * way - 2 + n, n)}, device_id_type=MESH
+        )
     for k in others:
         greet(pair, other(k))
     load_rhs(1, last).start()
@@ -231,12 +226,9 @@
 
     load_rhs(0, 1).wait()
     narrow(0)
-    pl.semaphore_wait(barrier, 2 * owners + parts - 1)
+    pl.semaphore_wait(barrier, owners + 1)
     for k in others:
         give_sides(0, k).start()
-    for s in range(owners):
-        for i in range(share):
-            give_edge(s, i).start()
     give_cols(0).start()
     give_cols(1).start()
 
@@ -271,9 +263,14 @@
         forward_item(level)
 
     load_rhs(1, last).wait()
-    each(1, AHEAD + 1, open_item)
+    open_item(1)
+    take_sides(0)
+    for i in range(share):
+        for j in range(parts):
+            for way in range(2):
+                give_row(y, 0, 0, i, j, way).start()
+    each(2, AHEAD + 1, open_item)
     each(AHEAD + 1, levels, narrow)
-    take_sides(0)
     for kind in range(2):
         load_cols(kind).wait()
         give_cols(kind).wait_recv()
@@ -292,19 +289,16 @@
                         tile = lax.select(found, tiles[level, p, i, k], tile)
                     chosen[i, p, d] = tile
 
-    def early(sweep, level, source, own):
-        for i in range(share):
-            first = own[source, i, 0:parts].reshape(parts * sides, block)
-            second = own[source, i, parts:owners].reshape(parts * sides, block)
-            for p in range(2):
-                start = y[level, i, p * parts : (p + 1) * parts].reshape(parts * sides, block)
-                terms = product(first, chosen[i, p, 1 - p]) + product(second, chosen[i, p, 2 - p])
-                acc[i, p] = (start.astype(jnp.float32) - terms).reshape(parts, sides, block)
-
-    def late(own, sweep, source, i, j):
+    def step(own, sweep, level, source, i, j):
+        first = own[source, i, j]
+        second = own[source, i, parts + j]
+        kept = []
+        for p in range(2):
+            terms = product(first, chosen[i, p, 1 - p]) + product(second, chosen[i, p, 2 - p])
+            kept.append(y[level, i, p * parts + j].astype(jnp.float32) - terms)
         take_rows(sweep, source, i, j)
-        low = acc[i, 0, j] - product(halo[sweep, source, i, j, 1], chosen[i, 0, 0])
-        high = acc[i, 1, j] - product(halo[sweep, source, i, j, 0], chosen[i, 1, 2])
+        low = kept[0] - product(halo[sweep, source, i, j, 1], chosen[i, 0, 0])
+        high = kept[1] - product(halo[sweep, source, i, j, 0], chosen[i, 1, 2])
         return low.astype(jnp.bfloat16), high.astype(jnp.bfloat16)
 
     def arrive_forward(level):
@@ -314,10 +308,9 @@
     def forward(level):
         arrive_forward(level)
         choose(0, level, level - 1, lower_v)
-        early(0, level, level - 1, y)
         for i in range(share):
             for j in range(parts):
-                low, high = late(y, 0, level - 1, i, j)
+                low, high = step(y, 0, level, level - 1, i, j)
                 y[level, i, j] = low
                 y[level, i, parts + j] = high
                 for way in range(2):
@@ -330,33 +323,26 @@
         x[level, i, j] = product(low, inverse_v[level, 0, i]).astype(jnp.bfloat16)
         x[level, i, parts + j] = product(high, inverse_v[level, 1, i]).astype(jnp.bfloat16)
 
-    def leave(level):
-        for k in others:
-            give_out(level, k).start()
-        keep_out(level).start()
-
     arrive_forward(last)
     give_tiles(2, last).wait_recv()
     choose(0, last, last - 1, lower_v)
-    early(0, last, last - 1, y)
     for i in range(share):
         for j in range(parts):
-            low, high = late(y, 0, last - 1, i, j)
+            low, high = step(y, 0, last, last - 1, i, j)
             solve(last, i, j, low, high)
             for way in range(2):
                 give_row(x, 1, last, i, j, way).start()
+            leave_piece(last, i, j)
     ahead_forward(last)
-    leave(last)
 
     def backward(turn):
         level = last - turn
         give_tiles(1, level).wait_recv()
         give_tiles(2, level).wait_recv()
         choose(1, level, level + 1, upper_v)
-        early(1, level, level + 1, x)
         for i in range(share):
             for j in range(parts):
-                low, high = late(x, 1, level + 1, i, j)
+                low, high = step(x, 1, level, level + 1, i, j)
                 solve(level, i, j, low, high)
 
                 @pl.when(level > 0)
@@ -364,17 +350,17 @@
                     for way in range(2):
                         give_row(x, 1, level, i, j, way).start()
 
+                leave_piece(level, i, j)
+
         ahead_backward(turn)
-        leave(level)
 
     each(1, levels, backward)
 
     for kind in range(2):
         give_cols(kind).wait_send()
-    edges_given()
     sides_given()
-    rows_given(y, 0, last - 1)
-    rows_given(x, 1, last)
+    rows_given(y, 0)
+    rows_given(x, 1)
     for kind in range(3):
         tiles_given(kind)
     outs_done()
@@ -407,7 +393,6 @@
             tiles,
             pltpu.VMEM((levels, 2, share, block, block), half),
             pltpu.VMEM((share, 2, 3, block, block), half),
-            pltpu.VMEM((share, 2, parts, sides, block), jnp.float32),
             own,
             own,
             pltpu.VMEM((2, levels, share, parts, 2, sides, block), half),
@@ -418,7 +403,6 @@
             dma((3, levels)),
             dma((1,)),
             dma((levels,)),
-            dma((1,)),
             dma((2,)),
             dma((2, share, parts)),
             dma((3,)),

time: 79 us -> 74.5 us (0.943)
  Pallas kernels: 76.3 us -> 71.9 us
    pallas_call x1, Pallas kernels: 76.3 us -> 71.9 us  [on_device(): pl.pallas_call(functools.partial(sweep_kernel, n, parts), out_shape=jax.S...]
    unnamed x5 -> x1, local copies, waits for them, and re-layouts: 2.39 us -> 2.26 us
where the time goes in v3:
time: 74.5 us; the launch traced here: 74.2 us
  Pallas kernels  71.9 us (97%)
  local copies, waits for them, and re-layouts  2.26 us (3%)
    pallas_call x1, Pallas kernels, on_device(): pl.pallas_call(functools.partial(sweep_kernel, n, parts), out_shape=jax.S...  71.9 us
    unnamed x1, local copies, waits for them, and re-layouts  2.26 us

profile of v3, /device:TPU:0, one launch (start us, length us, event | category | flops | bytes accessed | tf_op | source)
XLA Modules:
  0.0 74.2 jit_solution(6978172941844496454)
XLA Ops:
  0.0 71.9 %shard_map.64 = bf16[8,8,64,128]{3,2,1,0:T(8,128)(2,1)} custom-call(s32[8,3,1,8]{3,2,1,0:T(1,128)} %bitcast.14, s32[8,3,1,8]{3,2,1,0:T(1,128)} %bitcast.15, f32[8,8,64,128]{3,2,1,0:T(8,128)} %bitcast.12, bf16[8,8,3,128,128]{4,3,2,1,0:T(8,128)(2,1)} %bitcast.9, bf16[8,8,3,128,128]{4,3,2,1,0:T(8,128)(2,1)} %bitcast.10, bf16[8,8,128,128]{3,2,1,0:T(8,128)(2,1)} %bitcast.13), custom_call_target="tpu_custom_call" | custom-call | tf_op jit(solution)/shard_map/pallas_call | solution.py:383
  72.0 2.3 %copy.9 = bf16[8,8,1,64,128]{4,3,2,1,0:T(8,128)(2,1)} copy(bf16[8,8,1,64,128]{4,3,2,1,0:T(8,128)(2,1)} %bitcast.11) | data formatting | bytes 2097152

commit v4 on v3

--- a/solution.py
+++ b/solution.py
@@ -10,6 +10,7 @@
 MESH = pl.DeviceIdType.MESH
 VMEM_LIMIT = 67043328
 AHEAD = 4
+SPLIT = 2
 
 
 def product(x, tile):
@@ -60,6 +61,11 @@
     owner = half * parts + part
     mine = owner * share
     others = range(1, owners)
+    part_size = sides // SPLIT
+    pieces = [(j, pl.ds(u * part_size, part_size)) for j in range(parts) for u in range(SPLIT)]
+
+    def ready(j, span):
+        return j * SPLIT + span.start // part_size
 
     def other(k):
         return lax.rem(owner + k, owners)
@@ -144,19 +150,19 @@
     def turn_of(sweep, level):
         return lax.rem(level if sweep == 0 else 2 * last - level, 2)
 
-    def give_row(own, sweep, level, i, j, way):
+    def give_row(own, sweep, level, i, j, span, way):
         return remote(
-            own.at[level, i, way * parts + j],
-            halo.at[sweep, level, i, j, way],
+            own.at[level, i, way * parts + j, span],
+            halo.at[sweep, level, i, j, way, span],
             row_send.at[sweep],
-            row_recv.at[turn_of(sweep, level), i, j],
+            row_recv.at[turn_of(sweep, level), i, ready(j, span)],
             {"blk": lax.rem(me + 4 * way - 2 + n, n)},
         )
 
-    def take_rows(sweep, level, i, j):
-        whole = halo.at[sweep, level, i, j]
+    def take_rows(sweep, level, i, j, span):
+        whole = halo.at[sweep, level, i, j, :, span]
         remote(
-            whole, whole, row_send.at[sweep], row_recv.at[turn_of(sweep, level), i, j], {"blk": partner}
+            whole, whole, row_send.at[sweep], row_recv.at[turn_of(sweep, level), i, ready(j, span)], {"blk": partner}
         ).wait_recv()
 
     def rows_given(own, sweep):
@@ -266,9 +272,9 @@
     open_item(1)
     take_sides(0)
     for i in range(share):
-        for j in range(parts):
+        for j, span in pieces:
             for way in range(2):
-                give_row(y, 0, 0, i, j, way).start()
+                give_row(y, 0, 0, i, j, span, way).start()
     each(2, AHEAD + 1, open_item)
     each(AHEAD + 1, levels, narrow)
     for kind in range(2):
@@ -289,17 +295,30 @@
                         tile = lax.select(found, tiles[level, p, i, k], tile)
                     chosen[i, p, d] = tile
 
-    def step(own, sweep, level, source, i, j):
-        first = own[source, i, j]
-        second = own[source, i, parts + j]
+    def step(own, sweep, level, source, i, j, span):
+        first = own[source, i, j, span]
+        second = own[source, i, parts + j, span]
         kept = []
         for p in range(2):
             terms = product(first, chosen[i, p, 1 - p]) + product(second, chosen[i, p, 2 - p])
-            kept.append(y[level, i, p * parts + j].astype(jnp.float32) - terms)
-        take_rows(sweep, source, i, j)
-        low = kept[0] - product(halo[sweep, source, i, j, 1], chosen[i, 0, 0])
-        high = kept[1] - product(halo[sweep, source, i, j, 0], chosen[i, 1, 2])
+            kept.append(y[level, i, p * parts + j, span].astype(jnp.float32) - terms)
+        if sweep == 1:
+            kept = [product(kept[p].astype(jnp.bfloat16), inverse_v[level, p, i]) for p in range(2)]
+        take_rows(sweep, source, i, j, span)
+        low = kept[0] - product(halo[sweep, source, i, j, 1, span], chosen[i, 0, 0])
+        high = kept[1] - product(halo[sweep, source, i, j, 0, span], chosen[i, 1, 2])
         return low.astype(jnp.bfloat16), high.astype(jnp.bfloat16)
+
+    def join(level):
+        for i in range(share):
+            for p in range(2):
+                both = lax.dot_general(
+                    inverse_v[level, p, i],
+                    chosen[i, p, 2 * p],
+                    (((1,), (0,)), ((), ())),
+                    preferred_element_type=jnp.float32,
+                )
+                chosen[i, p, 2 * p] = both.astype(jnp.bfloat16)
 
     def arrive_forward(level):
         take_sides(level)
@@ -309,30 +328,31 @@
         arrive_forward(level)
         choose(0, level, level - 1, lower_v)
         for i in range(share):
-            for j in range(parts):
-                low, high = step(y, 0, level, level - 1, i, j)
-                y[level, i, j] = low
-                y[level, i, parts + j] = high
+            for j, span in pieces:
+                low, high = step(y, 0, level, level - 1, i, j, span)
+                y[level, i, j, span] = low
+                y[level, i, parts + j, span] = high
                 for way in range(2):
-                    give_row(y, 0, level, i, j, way).start()
+                    give_row(y, 0, level, i, j, span, way).start()
         ahead_forward(level)
 
     each(1, last, forward)
 
-    def solve(level, i, j, low, high):
-        x[level, i, j] = product(low, inverse_v[level, 0, i]).astype(jnp.bfloat16)
-        x[level, i, parts + j] = product(high, inverse_v[level, 1, i]).astype(jnp.bfloat16)
+    def solve(level, i, j, span, low, high):
+        x[level, i, j, span] = product(low, inverse_v[level, 0, i]).astype(jnp.bfloat16)
+        x[level, i, parts + j, span] = product(high, inverse_v[level, 1, i]).astype(jnp.bfloat16)
 
     arrive_forward(last)
     give_tiles(2, last).wait_recv()
     choose(0, last, last - 1, lower_v)
     for i in range(share):
-        for j in range(parts):
-            low, high = step(y, 0, last, last - 1, i, j)
-            solve(last, i, j, low, high)
+        for j, span in pieces:
+            low, high = step(y, 0, last, last - 1, i, j, span)
+            solve(last, i, j, span, low, high)
             for way in range(2):
-                give_row(x, 1, last, i, j, way).start()
-            leave_piece(last, i, j)
+                give_row(x, 1, last, i, j, span, way).start()
+            if span.start + part_size == sides:
+                leave_piece(last, i, j)
     ahead_forward(last)
 
     def backward(turn):
@@ -340,17 +360,20 @@
         give_tiles(1, level).wait_recv()
         give_tiles(2, level).wait_recv()
         choose(1, level, level + 1, upper_v)
+        join(level)
         for i in range(share):
-            for j in range(parts):
-                low, high = step(x, 1, level, level + 1, i, j)
-                solve(level, i, j, low, high)
+            for j, span in pieces:
+                low, high = step(x, 1, level, level + 1, i, j, span)
+                x[level, i, j, span] = low
+                x[level, i, parts + j, span] = high
 
                 @pl.when(level > 0)
                 def _():
                     for way in range(2):
-                        give_row(x, 1, level, i, j, way).start()
-
-                leave_piece(level, i, j)
+                        give_row(x, 1, level, i, j, span, way).start()
+
+                if span.start + part_size == sides:
+                    leave_piece(level, i, j)
 
         ahead_backward(turn)
 
@@ -404,7 +427,7 @@
             dma((1,)),
             dma((levels,)),
             dma((2,)),
-            dma((2, share, parts)),
+            dma((2, share, parts * SPLIT)),
             dma((3,)),
         ],
         compiler_params=pltpu.CompilerParams(collective_id=0, has_side_effects=True, vmem_limit_bytes=VMEM_LIMIT),

time: 74.5 us -> 72.5 us (0.973)
  Pallas kernels: 71.9 us -> 70.1 us
    pallas_call x1, Pallas kernels: 71.9 us -> 70.1 us  [on_device(): pl.pallas_call(functools.partial(sweep_kernel, n, parts), out_shape=jax.S...]
where the time goes in v4:
time: 72.5 us; the launch traced here: 72.4 us
  Pallas kernels  70.1 us (97%)
  local copies, waits for them, and re-layouts  2.26 us (3%)
    pallas_call x1, Pallas kernels, on_device(): pl.pallas_call(functools.partial(sweep_kernel, n, parts), out_shape=jax.S...  70.1 us
    unnamed x1, local copies, waits for them, and re-layouts  2.26 us

profile of v4, /device:TPU:0, one launch (start us, length us, event | category | flops | bytes accessed | tf_op | source)
XLA Modules:
  0.0 72.4 jit_solution(13456762102999610985)
XLA Ops:
  0.0 70.1 %shard_map.64 = bf16[8,8,64,128]{3,2,1,0:T(8,128)(2,1)} custom-call(s32[8,3,1,8]{3,2,1,0:T(1,128)} %bitcast.14, s32[8,3,1,8]{3,2,1,0:T(1,128)} %bitcast.15, f32[8,8,64,128]{3,2,1,0:T(8,128)} %bitcast.12, bf16[8,8,3,128,128]{4,3,2,1,0:T(8,128)(2,1)} %bitcast.9, bf16[8,8,3,128,128]{4,3,2,1,0:T(8,128)(2,1)} %bitcast.10, bf16[8,8,128,128]{3,2,1,0:T(8,128)(2,1)} %bitcast.13), custom_call_target="tpu_custom_call" | custom-call | tf_op jit(solution)/shard_map/pallas_call | solution.py:406
  70.1 2.3 %copy.9 = bf16[8,8,1,64,128]{4,3,2,1,0:T(8,128)(2,1)} copy(bf16[8,8,1,64,128]{4,3,2,1,0:T(8,128)(2,1)} %bitcast.11) | data formatting | bytes 2097152

commit v5 on v4

--- a/solution.py
+++ b/solution.py
@@ -239,9 +239,9 @@
     give_cols(1).start()
 
     def forward_item(level):
+        give_tiles(0, level).start()
         for k in others:
             give_sides(level, k).start()
-        give_tiles(0, level).start()
 
     def backward_item(level):
         @pl.when(level < last)

time: 72.5 us -> 71.7 us (0.989)
  Pallas kernels: 70.1 us -> 69.1 us
    pallas_call x1, Pallas kernels: 70.1 us -> 69.1 us  [on_device(): pl.pallas_call(functools.partial(sweep_kernel, n, parts), out_shape=jax.S...]
where the time goes in v5:
time: 71.7 us; the launch traced here: 71.4 us
  Pallas kernels  69.1 us (96%)
  local copies, waits for them, and re-layouts  2.26 us (3%)
    pallas_call x1, Pallas kernels, on_device(): pl.pallas_call(functools.partial(sweep_kernel, n, parts), out_shape=jax.S...  69.1 us
    unnamed x1, local copies, waits for them, and re-layouts  2.26 us

profile of v5, /device:TPU:0, one launch (start us, length us, event | category | flops | bytes accessed | tf_op | source)
XLA Modules:
  0.0 71.4 jit_solution(8425127829571999332)
XLA Ops:
  0.0 69.1 %shard_map.64 = bf16[8,8,64,128]{3,2,1,0:T(8,128)(2,1)} custom-call(s32[8,3,1,8]{3,2,1,0:T(1,128)} %bitcast.14, s32[8,3,1,8]{3,2,1,0:T(1,128)} %bitcast.15, f32[8,8,64,128]{3,2,1,0:T(8,128)} %bitcast.12, bf16[8,8,3,128,128]{4,3,2,1,0:T(8,128)(2,1)} %bitcast.9, bf16[8,8,3,128,128]{4,3,2,1,0:T(8,128)(2,1)} %bitcast.10, bf16[8,8,128,128]{3,2,1,0:T(8,128)(2,1)} %bitcast.13), custom_call_target="tpu_custom_call" | custom-call | tf_op jit(solution)/shard_map/pallas_call | solution.py:406
  69.1 2.3 %copy.9 = bf16[8,8,1,64,128]{4,3,2,1,0:T(8,128)(2,1)} copy(bf16[8,8,1,64,128]{4,3,2,1,0:T(8,128)(2,1)} %bitcast.11) | data formatting | bytes 2097152
